TPU v7x, 32 devices: a whole 2x2x4 slice. The times are simulated.
32 devices in a mesh: row: 2 (over x), col: 16 (over z, y, core).
Axes of the slice: x: 2, y: 2, z: 4, core: 2. Of those that a mesh axis runs over, the one named last changes fastest.
Arguments:
- features: bfloat16 [8192, 256], P(('row', 'col')), may hold values from -6 to 6
- weight: bfloat16 [256, 128], replicated, may hold values from -0.375 to 0.375
- tiles: bfloat16 [2, 16, 320, 128, 128], P('row', 'col'), may hold values from -0.0625 to 0.0625
- slot_tile_row: int32 [2, 16, 320], P('row', 'col'), may hold values from 0 to 3
- tile_cols: int32 [2, 16, 320], P('row', 'col'), may hold values from 0 to 31
- live_tiles: int32 [2, 16], P('row', 'col'), may hold values from 40 to 320, as said below
- cotangent: bfloat16 [8192, 128], P(('row', 'col')), may hold values from -6 to 6
Outputs:
- logits: bfloat16 [8192, 128], P(('row', 'col'))
- grad_features: bfloat16 [8192, 256], P(('row', 'col'))
- grad_weight: float32 [256, 128], replicated
Inputs may be any that keep to these rules, and one draw needn't show every extreme that they name: Slots of a block from live_tiles on are padding and not part of the adjacency; in every draw some block has all 320 slots live.
All inputs are finite; a program needn't handle non-finite values.
Results may differ from a plain program's by a relative error of at most 0.005.
Values may be sent and summed in bfloat16 or wider, within the bound.
A program may use at most 128 MiB of HBM per device.

v0:
```python
import math
import jax
import jax.numpy as jnp
from jax import lax
from jax.sharding import PartitionSpec as P


def per_device(features, weight, tiles, slot_tile_row, tile_cols, live_tiles, cotangent):
    tile_block = tiles[0, 0]
    slot_rows = slot_tile_row[0, 0]
    slot_cols = tile_cols[0, 0]
    live_count = live_tiles[0, 0]
    tile_extent = tile_block.shape[-1]
    slot_total = tile_block.shape[0]
    stretch_rows = features.shape[0]
    output_width = weight.shape[1]
    row_count = lax.axis_size("row")
    col_count = lax.axis_size("col")
    row_tiles = row_count * stretch_rows // tile_extent
    col_tiles = col_count * stretch_rows // tile_extent
    block_size = 64
    block_total = slot_total // block_size
    projected_group = jnp.dot(
        lax.all_gather(features, "col", axis=0, tiled=True),
        weight,
        preferred_element_type=jnp.float32,
    ).astype(jnp.bfloat16)
    proj_tiles = projected_group.reshape(col_tiles, tile_extent, output_width)

    def block_slice(first_slot):
        part_tiles = lax.dynamic_slice_in_dim(tile_block, first_slot, block_size, 0)
        part_rows = lax.dynamic_slice_in_dim(slot_rows, first_slot, block_size, 0)
        part_cols = lax.dynamic_slice_in_dim(slot_cols, first_slot, block_size, 0)
        live_mask = first_slot + jnp.arange(block_size, dtype=jnp.int32) < live_count
        return (part_tiles, part_rows, part_cols, live_mask)

    def forward_block(block_index, totals):
        part_tiles, part_rows, part_cols, live_mask = block_slice(block_index * block_size)
        inputs = proj_tiles[part_cols]
        products = jnp.einsum(
            "tab,tbf->taf", part_tiles, inputs, preferred_element_type=jnp.float32
        )
        segment_ids = jnp.where(live_mask, part_rows, row_tiles)
        summed = jax.ops.segment_sum(products, segment_ids, num_segments=row_tiles + 1)
        return totals + summed[:row_tiles]

    forward_totals = lax.fori_loop(
        0,
        block_total,
        forward_block,
        jnp.zeros((row_tiles, tile_extent, output_width), jnp.float32),
    )
    logits = lax.psum_scatter(
        forward_totals.reshape(row_tiles * tile_extent, output_width),
        "row",
        scatter_dimension=0,
        tiled=True,
    ).astype(jnp.bfloat16)
    cot_group = lax.all_gather(cotangent, "row", axis=0, tiled=True)
    cot_tiles = cot_group.reshape(row_tiles, tile_extent, output_width)

    def backward_block(block_index, totals):
        part_tiles, part_rows, part_cols, live_mask = block_slice(block_index * block_size)
        inputs = cot_tiles[part_rows]
        products = jnp.einsum(
            "tab,taf->tbf", part_tiles, inputs, preferred_element_type=jnp.float32
        )
        inside = live_mask & (part_cols >= 0) & (part_cols < col_tiles)
        segment_ids = jnp.where(inside, part_cols, col_tiles)
        summed = jax.ops.segment_sum(products, segment_ids, num_segments=col_tiles + 1)
        return totals + summed[:col_tiles]

    empty = jnp.zeros((col_tiles, tile_extent, output_width), jnp.float32)
    backward_totals = lax.fori_loop(0, block_total, backward_block, empty).reshape(
        col_tiles * tile_extent, output_width
    )
    back = lax.psum_scatter(backward_totals, "col", scatter_dimension=0, tiled=True)
    back_rounded = back.astype(jnp.bfloat16)
    grad_features = jnp.dot(back_rounded, weight.T, preferred_element_type=jnp.float32).astype(
        jnp.bfloat16
    )
    weight_term = lax.dot_general(
        features, back_rounded, (((0,), (0,)), ((), ())), preferred_element_type=jnp.float32
    )
    node_total = stretch_rows * row_count * col_count
    grad_weight = lax.psum(weight_term, ("row", "col")) / math.sqrt(node_total)
    return (logits, grad_features, grad_weight)


def solution(mesh):
    placed = (
        P(("row", "col"), None),
        P(),
        P("row", "col", None, None, None),
        P("row", "col", None),
        P("row", "col", None),
        P("row", "col"),
        P(("row", "col"), None),
    )
    return jax.shard_map(
        per_device,
        mesh=mesh,
        in_specs=placed,
        out_specs=(P(("row", "col"), None), P(("row", "col"), None), P()),
        check_vma=False,
    )
```

profile of v0, /device:TPU:0, one launch (start us, length us, event | category | flops | bytes accessed | tf_op | source)
XLA Modules:
  0.0 375.7 jit_solution(15768739046971264460)
XLA Ops:
  8.6 14.4 %copy.10 = bf16[1,1,320,128,128]{3,4,2,1,0:T(8,128)(2,1)} copy(bf16[1,1,320,128,128]{4,3,2,1,0:T(8,128)(2,1)} %param.13) | data formatting | bytes 20971520 | tf_op args[2]
  23.0 5.9 %all_gather.7 = bf16[512,128]{1,0:T(8,128)(2,1)S(1)} all-gather(bf16[256,128]{1,0:T(8,128)(2,1)S(1)} %copy-done.3), channel_id=1, replica_groups=mesh['row'=2,'col'=16] {'row'}, dimensions={0}, use_global_device_ids=true | all-gather | bytes 196608 | tf_op jit(solution)/shard_map/all_gather | solution.py:59
  28.9 90.2 %while.29 = (s32[]{:T(128)}, f32[32,128,128]{2,1,0:T(8,128)}, s32[]{:T(128)}, s32[320]{0:T(512)S(1)}, bf16[320,128,128]{1,2,0:T(8,128)(2,1)}, /*index=5*/s32[320...) while((s32[]{:T(128)}, f32[32,128,128]{2,1,0:T(8,128)}, ...), condition=%wide.region_6.7_spmd.clone, body=%wide.region_4.6_spmd.clone.sunk | while | flops 270534272 | bytes 33626048 | solution.py:74
  29.6 1.0 gather_fusion.1
  30.6 4.4 %fusion.25 = f32[64,128,128]{2,1,0:T(8,128)} fusion(bf16[64,128,128]{2,1,0:T(8,128)(2,1)S(1)} %gather_fusion.1, bf16[320,128,128]{1,2,0:T(8,128)(2,1)} %get-tuple-element.501, s32[]{:T(128)S(6)} %select_n.64), kind=kOutput, calls=%fused_computation.12.clone.1 | convolution fusion | flops 268435456 | bytes 8388612 | tf_op jit(solution)/shard_map/while/body/eval_jaxpr/tab,taf->tbf/dot_general | solution.py:65
  35.2 8.8 %scatter_fusion.1 = f32[33,128,128]{2,1,0:T(8,128)S(1)} fusion(f32[33,128,128]{2,1,0:T(8,128)S(1)} %broadcast.112, s32[64]{0:T(128)S(1)} %get-tuple-element.435, f32[64,128,128]{2,1,0:T(8,128)} %fusion.25), kind=kCustom, calls=%fused_computation.3.clone.clone.1 | custom fusion | flops 1048576 | bytes 12583168 | tf_op jit(solution)/shard_map/while/body/eval_jaxpr/scatter-add | solution.py:70
  44.0 1.6 slice_add_fusion.5
  46.4 1.0 gather_fusion.1
  47.4 4.4 %fusion.25 = f32[64,128,128]{2,1,0:T(8,128)} fusion(bf16[64,128,128]{2,1,0:T(8,128)(2,1)S(1)} %gather_fusion.1, bf16[320,128,128]{1,2,0:T(8,128)(2,1)} %get-tuple-element.501, s32[]{:T(128)S(6)} %select_n.64), kind=kOutput, calls=%fused_computation.12.clone.1 | convolution fusion | flops 268435456 | bytes 8388612 | tf_op jit(solution)/shard_map/while/body/eval_jaxpr/tab,taf->tbf/dot_general | solution.py:65
  52.0 8.8 %scatter_fusion.1 = f32[33,128,128]{2,1,0:T(8,128)S(1)} fusion(f32[33,128,128]{2,1,0:T(8,128)S(1)} %broadcast.112, s32[64]{0:T(128)S(1)} %get-tuple-element.435, f32[64,128,128]{2,1,0:T(8,128)} %fusion.25), kind=kCustom, calls=%fused_computation.3.clone.clone.1 | custom fusion | flops 1048576 | bytes 12583168 | tf_op jit(solution)/shard_map/while/body/eval_jaxpr/scatter-add | solution.py:70
  60.8 3.2 slice_add_fusion.5
  64.8 1.0 gather_fusion.1
  65.7 4.4 %fusion.25 = f32[64,128,128]{2,1,0:T(8,128)} fusion(bf16[64,128,128]{2,1,0:T(8,128)(2,1)S(1)} %gather_fusion.1, bf16[320,128,128]{1,2,0:T(8,128)(2,1)} %get-tuple-element.501, s32[]{:T(128)S(6)} %select_n.64), kind=kOutput, calls=%fused_computation.12.clone.1 | convolution fusion | flops 268435456 | bytes 8388612 | tf_op jit(solution)/shard_map/while/body/eval_jaxpr/tab,taf->tbf/dot_general | solution.py:65
  70.3 8.8 %scatter_fusion.1 = f32[33,128,128]{2,1,0:T(8,128)S(1)} fusion(f32[33,128,128]{2,1,0:T(8,128)S(1)} %broadcast.112, s32[64]{0:T(128)S(1)} %get-tuple-element.435, f32[64,128,128]{2,1,0:T(8,128)} %fusion.25), kind=kCustom, calls=%fused_computation.3.clone.clone.1 | custom fusion | flops 1048576 | bytes 12583168 | tf_op jit(solution)/shard_map/while/body/eval_jaxpr/scatter-add | solution.py:70
  79.2 3.2 slice_add_fusion.5
  83.1 1.0 gather_fusion.1
  84.1 4.4 %fusion.25 = f32[64,128,128]{2,1,0:T(8,128)} fusion(bf16[64,128,128]{2,1,0:T(8,128)(2,1)S(1)} %gather_fusion.1, bf16[320,128,128]{1,2,0:T(8,128)(2,1)} %get-tuple-element.501, s32[]{:T(128)S(6)} %select_n.64), kind=kOutput, calls=%fused_computation.12.clone.1 | convolution fusion | flops 268435456 | bytes 8388612 | tf_op jit(solution)/shard_map/while/body/eval_jaxpr/tab,taf->tbf/dot_general | solution.py:65
  88.7 8.8 %scatter_fusion.1 = f32[33,128,128]{2,1,0:T(8,128)S(1)} fusion(f32[33,128,128]{2,1,0:T(8,128)S(1)} %broadcast.112, s32[64]{0:T(128)S(1)} %get-tuple-element.435, f32[64,128,128]{2,1,0:T(8,128)} %fusion.25), kind=kCustom, calls=%fused_computation.3.clone.clone.1 | custom fusion | flops 1048576 | bytes 12583168 | tf_op jit(solution)/shard_map/while/body/eval_jaxpr/scatter-add | solution.py:70
  97.5 3.2 slice_add_fusion.5
  101.5 1.0 gather_fusion.1
  102.4 4.4 %fusion.25 = f32[64,128,128]{2,1,0:T(8,128)} fusion(bf16[64,128,128]{2,1,0:T(8,128)(2,1)S(1)} %gather_fusion.1, bf16[320,128,128]{1,2,0:T(8,128)(2,1)} %get-tuple-element.501, s32[]{:T(128)S(6)} %select_n.64), kind=kOutput, calls=%fused_computation.12.clone.1 | convolution fusion | flops 268435456 | bytes 8388612 | tf_op jit(solution)/shard_map/while/body/eval_jaxpr/tab,taf->tbf/dot_general | solution.py:65
  107.1 8.8 %scatter_fusion.1 = f32[33,128,128]{2,1,0:T(8,128)S(1)} fusion(f32[33,128,128]{2,1,0:T(8,128)S(1)} %broadcast.112, s32[64]{0:T(128)S(1)} %get-tuple-element.435, f32[64,128,128]{2,1,0:T(8,128)} %fusion.25), kind=kCustom, calls=%fused_computation.3.clone.clone.1 | custom fusion | flops 1048576 | bytes 12583168 | tf_op jit(solution)/shard_map/while/body/eval_jaxpr/scatter-add | solution.py:70
  115.9 3.2 slice_add_fusion.5
  119.9 62.9 %reduce-scatter.5.cloned.1.call-done = f32[256,128]{1,0:T(8,128)} async-done(((f32[4096,128]{1,0:T(8,128)}), f32[256,128]{1,0:T(8,128)}) %reduce-scatter.5.cloned.1.call-update) | async-done | bytes 131088 | tf_op jit(solution)/shard_map/reduce_scatter | solution.py:77
  182.8 1.8 convolution_bitcast_fusion
  184.6 40.8 %all-gather.2.cloned.1.call-done = bf16[4096,256]{1,0:T(8,128)(2,1)} async-done(((bf16[256,256]{1,0:T(8,128)(2,1)}), bf16[4096,256]{1,0:T(8,128)(2,1)}) %all-gather.2.cloned.1.call-update) | async-done | bytes 2097168 | tf_op jit(solution)/shard_map/all_gather | solution.py:24
  225.4 2.3 convolution_convert_fusion
  227.7 74.2 %while.28 = (s32[]{:T(128)}, f32[4,128,128]{2,1,0:T(8,128)S(1)}, s32[]{:T(128)}, s32[320]{0:T(512)S(1)}, bf16[320,128,128]{2,1,0:T(8,128)(2,1)}, /*index=5*/s32[...) while((s32[]{:T(128)}, f32[4,128,128]{2,1,0:T(8,128)S(1)}, ...), condition=%wide.region_2.3_spmd.clone, body=%wide.region_0.2_spmd.clone.sunk | while | flops 269616512 | bytes 26286016 | solution.py:47
  228.4 1.0 gather_fusion
  229.4 4.2 %fusion.22 = f32[64,128,128]{2,1,0:T(8,128)} fusion(bf16[64,128,128]{2,1,0:T(8,128)(2,1)S(1)} %gather_fusion, bf16[320,128,128]{2,1,0:T(8,128)(2,1)} %get-tuple-element.465, s32[]{:T(128)S(6)} %select_n.62), kind=kOutput, calls=%fused_computation.4.clone.1 | convolution fusion | flops 268435456 | bytes 8388612 | tf_op jit(solution)/shard_map/while/body/eval_jaxpr/tab,tbf->taf/dot_general | solution.py:40
  233.7 8.8 %scatter_fusion = f32[5,128,128]{2,1,0:T(8,128)S(1)} fusion(f32[5,128,128]{2,1,0:T(8,128)S(1)} %broadcast.105, s32[64]{0:T(128)S(1)} %get-tuple-element.426, f32[64,128,128]{2,1,0:T(8,128)} %fusion.22), kind=kCustom, calls=%fused_computation.2.clone.clone.1 | custom fusion | flops 1048576 | bytes 12583168 | tf_op jit(solution)/shard_map/while/body/eval_jaxpr/scatter-add | solution.py:44
  243.3 1.0 gather_fusion
  244.2 4.2 %fusion.22 = f32[64,128,128]{2,1,0:T(8,128)} fusion(bf16[64,128,128]{2,1,0:T(8,128)(2,1)S(1)} %gather_fusion, bf16[320,128,128]{2,1,0:T(8,128)(2,1)} %get-tuple-element.465, s32[]{:T(128)S(6)} %select_n.62), kind=kOutput, calls=%fused_computation.4.clone.1 | convolution fusion | flops 268435456 | bytes 8388612 | tf_op jit(solution)/shard_map/while/body/eval_jaxpr/tab,tbf->taf/dot_general | solution.py:40
  248.5 8.8 %scatter_fusion = f32[5,128,128]{2,1,0:T(8,128)S(1)} fusion(f32[5,128,128]{2,1,0:T(8,128)S(1)} %broadcast.105, s32[64]{0:T(128)S(1)} %get-tuple-element.426, f32[64,128,128]{2,1,0:T(8,128)} %fusion.22), kind=kCustom, calls=%fused_computation.2.clone.clone.1 | custom fusion | flops 1048576 | bytes 12583168 | tf_op jit(solution)/shard_map/while/body/eval_jaxpr/scatter-add | solution.py:44
  258.1 1.0 gather_fusion
  259.1 4.2 %fusion.22 = f32[64,128,128]{2,1,0:T(8,128)} fusion(bf16[64,128,128]{2,1,0:T(8,128)(2,1)S(1)} %gather_fusion, bf16[320,128,128]{2,1,0:T(8,128)(2,1)} %get-tuple-element.465, s32[]{:T(128)S(6)} %select_n.62), kind=kOutput, calls=%fused_computation.4.clone.1 | convolution fusion | flops 268435456 | bytes 8388612 | tf_op jit(solution)/shard_map/while/body/eval_jaxpr/tab,tbf->taf/dot_general | solution.py:40
  263.4 8.8 %scatter_fusion = f32[5,128,128]{2,1,0:T(8,128)S(1)} fusion(f32[5,128,128]{2,1,0:T(8,128)S(1)} %broadcast.105, s32[64]{0:T(128)S(1)} %get-tuple-element.426, f32[64,128,128]{2,1,0:T(8,128)} %fusion.22), kind=kCustom, calls=%fused_computation.2.clone.clone.1 | custom fusion | flops 1048576 | bytes 12583168 | tf_op jit(solution)/shard_map/while/body/eval_jaxpr/scatter-add | solution.py:44
  273.0 1.0 gather_fusion
  273.9 4.2 %fusion.22 = f32[64,128,128]{2,1,0:T(8,128)} fusion(bf16[64,128,128]{2,1,0:T(8,128)(2,1)S(1)} %gather_fusion, bf16[320,128,128]{2,1,0:T(8,128)(2,1)} %get-tuple-element.465, s32[]{:T(128)S(6)} %select_n.62), kind=kOutput, calls=%fused_computation.4.clone.1 | convolution fusion | flops 268435456 | bytes 8388612 | tf_op jit(solution)/shard_map/while/body/eval_jaxpr/tab,tbf->taf/dot_general | solution.py:40
  278.2 8.8 %scatter_fusion = f32[5,128,128]{2,1,0:T(8,128)S(1)} fusion(f32[5,128,128]{2,1,0:T(8,128)S(1)} %broadcast.105, s32[64]{0:T(128)S(1)} %get-tuple-element.426, f32[64,128,128]{2,1,0:T(8,128)} %fusion.22), kind=kCustom, calls=%fused_computation.2.clone.clone.1 | custom fusion | flops 1048576 | bytes 12583168 | tf_op jit(solution)/shard_map/while/body/eval_jaxpr/scatter-add | solution.py:44
  287.8 1.0 gather_fusion
  288.8 4.2 %fusion.22 = f32[64,128,128]{2,1,0:T(8,128)} fusion(bf16[64,128,128]{2,1,0:T(8,128)(2,1)S(1)} %gather_fusion, bf16[320,128,128]{2,1,0:T(8,128)(2,1)} %get-tuple-element.465, s32[]{:T(128)S(6)} %select_n.62), kind=kOutput, calls=%fused_computation.4.clone.1 | convolution fusion | flops 268435456 | bytes 8388612 | tf_op jit(solution)/shard_map/while/body/eval_jaxpr/tab,tbf->taf/dot_general | solution.py:40
  293.1 8.8 %scatter_fusion = f32[5,128,128]{2,1,0:T(8,128)S(1)} fusion(f32[5,128,128]{2,1,0:T(8,128)S(1)} %broadcast.105, s32[64]{0:T(128)S(1)} %get-tuple-element.426, f32[64,128,128]{2,1,0:T(8,128)} %fusion.22), kind=kCustom, calls=%fused_computation.2.clone.clone.1 | custom fusion | flops 1048576 | bytes 12583168 | tf_op jit(solution)/shard_map/while/body/eval_jaxpr/scatter-add | solution.py:44
  302.7 1.8 convolution_convert_fusion.1
  304.4 50.3 %all-reduce.2.cloned.1.call-done = f32[256,128]{0,1:T(8,128)} async-done(((f32[256,128]{0,1:T(8,128)}), f32[256,128]{0,1:T(8,128)}) %all-reduce.2.cloned.1.call-update) | async-done | bytes 131088 | tf_op jit(solution)/shard_map/psum | solution.py:86
  354.7 0.9 broadcast_multiply_fusion
  356.4 11.2 %reduce-scatter.3.cloned.1.call-done = f32[256,128]{1,0:T(8,128)} async-done(((f32[512,128]{1,0:T(8,128)}), f32[256,128]{1,0:T(8,128)}) %reduce-scatter.3.cloned.1.call-update) | async-done | bytes 131088 | tf_op jit(solution)/shard_map/reduce_scatter | solution.py:53
  367.6 1.5 convert_element_type.13
  (56 shorter events, 12.8 us)
Async XLA Ops:
  7.2 218.2 %copy-start = (bf16[256,128]{1,0:T(8,128)(2,1)S(1)}, bf16[256,128]{1,0:T(8,128)(2,1)}, u32[]{:S(2)}) copy-start(bf16[256,128]{1,0:T(8,128)(2,1)} %param.12) | copy-start | bytes 196612
  7.2 175.6 %reduce-scatter.5.cloned.1.call-start = ((), (), s32[]{:S(2)}) async-start(), calls=%async_computation.4 | async-start | bytes 2228224 | tf_op jit(solution)/shard_map/reduce_scatter | solution.py:77
  8.6 14.4 %copy-start.3 = (bf16[256,128]{1,0:T(8,128)(2,1)S(1)}, bf16[256,128]{1,0:T(8,128)(2,1)}, u32[]{:S(2)}) copy-start(bf16[256,128]{1,0:T(8,128)(2,1)} %param.17) | copy-start | bytes 196612
  119.1 63.7 %copy-start.2 = (bf16[256,256]{1,0:T(8,128)(2,1)S(1)}, bf16[256,256]{1,0:T(8,128)(2,1)}, u32[]{:S(2)}) copy-start(bf16[256,256]{1,0:T(8,128)(2,1)} %param.11) | copy-start | bytes 393220
  119.1 106.3 %all-gather.2.cloned.1.call-start = ((), (), s32[]{:S(2)}) async-start(), calls=%async_computation.2 | async-start | bytes 2228224 | tf_op jit(solution)/shard_map/all_gather | solution.py:24
  119.9 234.9 %all-reduce.2.cloned.1.call-start = ((), (), s32[]{:S(2)}) async-start(), calls=%async_computation.5 | async-start | bytes 262144 | tf_op jit(solution)/shard_map/psum | solution.py:86
  184.6 183.1 %reduce-scatter.3.cloned.1.call-start = ((), (), s32[]{:S(2)}) async-start(), calls=%async_computation.3 | async-start | bytes 393216 | tf_op jit(solution)/shard_map/reduce_scatter | solution.py:53
  301.9 0.7 copy-start.1
Sparse Core Ops, SparseCore 0:
  119.3 63.4 reduce-scatter.4
  185.0 40.3 all-gather.1
  231.5 123.1 all-reduce.1
  356.8 10.7 reduce-scatter.2
where the time goes:
time: 378 us; the launch traced here: 376 us
  waiting for transfers between devices  166 us (44%)
  other arithmetic  114 us (30%)
  matrix products  48.8 us (13%)
  local copies, waits for them, and re-layouts  26.7 us (7%)
  between operations  13.8 us (4%)
  blocking collectives  5.85 us (2%)
    reduce_scatter x1, waiting for transfers between devices, per_device(): lax.psum_scatter(backward_totals, 'col', scatter_dimension=0, tiled=True)  62.9 us
    psum x1, waiting for transfers between devices, per_device(): grad_weight = lax.psum(weight_term, ('row', 'col')) / math.sqrt(node_total)  50.3 us
    scatter-add x5, other arithmetic, backward_block(): jax.ops.segment_sum(products, segment_ids, num_segments=col_tiles + 1)  44 us
    scatter-add x5, other arithmetic, forward_block(): jax.ops.segment_sum(products, segment_ids, num_segments=row_tiles + 1)  43.9 us
    all_gather x1, waiting for transfers between devices, per_device(): lax.all_gather(features, 'col', axis=0, tiled=True)  40.8 us
    dot_general x5, matrix products, backward_block(): jnp.einsum('tab,taf->tbf', part_tiles, inputs, preferred_element_type=jnp...  21.9 us
    dot_general x5, matrix products, forward_block(): jnp.einsum('tab,tbf->taf', part_tiles, inputs, preferred_element_type=jnp...  21.1 us
    unnamed x10, local copies, waits for them, and re-layouts  15.9 us
  transfers between devices with their start and end apart: 4, of which 4 were waited for; matrix products, arithmetic and copies ran while one was open for 22% of the time, Pallas kernels for 0%

commit v1 on v0

--- a/solution.py
+++ b/solution.py
@@ -83,7 +83,12 @@
         features, back_rounded, (((0,), (0,)), ((), ())), preferred_element_type=jnp.float32
     )
     node_total = stretch_rows * row_count * col_count
-    grad_weight = lax.psum(weight_term, ("row", "col")) / math.sqrt(node_total)
+
+    def turn_sections_for(block_here, axis_key):
+        outcome_arr = jax.lax.all_gather(block_here, axis_key)
+        return jnp.sum(outcome_arr, 0)
+
+    grad_weight = turn_sections_for(weight_term, ("row", "col")) / math.sqrt(node_total)
     return (logits, grad_features, grad_weight)
 
 

time: 378 us -> 293 us (0.78)
  waiting for transfers between devices: 166 us -> 76 us
    all_gather x0 -> x1, waiting for transfers between devices: none -> 64.9 us  [turn_sections_for(): outcome_arr = jax.lax.all_gather(block_here, axis_key)]
    reduce_scatter x1, waiting for transfers between devices: 62.9 us -> 0.02 us  [per_device(): lax.psum_scatter(backward_totals, 'col', scatter_dimension=0, tiled=True)]
    psum x1 -> x0, waiting for transfers between devices: 50.3 us -> none  [per_device(): grad_weight = lax.psum(weight_term, ('row', 'col')) / math.sqrt(node_total)]
    all_gather x1, waiting for transfers between devices: 40.8 us -> 0.02 us  [per_device(): lax.all_gather(features, 'col', axis=0, tiled=True)]
    unnamed x10 -> x9, local copies, waits for them, and re-layouts: 15.9 us -> 19.4 us
  transfers between devices with their start and end apart: 4 -> 4, of which waited for: 4 -> 2; matrix products, arithmetic and copies ran while one was open for 22% -> 65% of each run, Pallas kernels for 0% -> 0%
where the time goes in v1:
time: 293 us; the launch traced here: 290 us
  other arithmetic  114 us (39%)
  waiting for transfers between devices  76 us (26%)
  matrix products  49 us (17%)
  local copies, waits for them, and re-layouts  30.2 us (10%)
  between operations  13.9 us (5%)
  blocking collectives  5.85 us (2%)
    all_gather x1, waiting for transfers between devices, turn_sections_for(): outcome_arr = jax.lax.all_gather(block_here, axis_key)  64.9 us
    scatter-add x5, other arithmetic, forward_block(): jax.ops.segment_sum(products, segment_ids, num_segments=row_tiles + 1)  44.1 us
    scatter-add x5, other arithmetic, backward_block(): jax.ops.segment_sum(products, segment_ids, num_segments=col_tiles + 1)  44 us
    dot_general x5, matrix products, backward_block(): jnp.einsum('tab,taf->tbf', part_tiles, inputs, preferred_element_type=jnp...  21.9 us
    dot_general x5, matrix products, forward_block(): jnp.einsum('tab,tbf->taf', part_tiles, inputs, preferred_element_type=jnp...  21.2 us
    unnamed x9, local copies, waits for them, and re-layouts  19.4 us
    add x5, other arithmetic, backward_block(): return totals + summed[:col_tiles]  14.6 us
    reduce_scatter x1, waiting for transfers between devices, per_device(): lax.psum_scatter(forward_totals.reshape(row_tiles * tile_extent, output_w...  10.3 us
  transfers between devices with their start and end apart: 4, of which 2 were waited for; matrix products, arithmetic and copies ran while one was open for 65% of the time, Pallas kernels for 0%

profile of v1, /device:TPU:0, one launch (start us, length us, event | category | flops | bytes accessed | tf_op | source)
XLA Modules:
  0.0 289.8 jit_solution(16920349037195931348)
XLA Ops:
  9.4 14.4 %copy.12 = bf16[1,1,320,128,128]{3,4,2,1,0:T(8,128)(2,1)} copy(bf16[1,1,320,128,128]{4,3,2,1,0:T(8,128)(2,1)} %param.13) | data formatting | bytes 20971520 | tf_op args[2]
  23.8 5.9 %all_gather.13 = bf16[512,128]{1,0:T(8,128)(2,1)S(1)} all-gather(bf16[256,128]{1,0:T(8,128)(2,1)S(1)} %copy-done.2), channel_id=1, replica_groups=mesh['row'=2,'col'=16] {'row'}, dimensions={0}, use_global_device_ids=true | all-gather | bytes 196608 | tf_op jit(solution)/shard_map/all_gather | solution.py:59
  29.6 90.3 %while.29 = (s32[]{:T(128)}, f32[32,128,128]{2,1,0:T(8,128)}, s32[]{:T(128)}, s32[320]{0:T(512)S(1)}, bf16[320,128,128]{1,2,0:T(8,128)(2,1)}, /*index=5*/s32[320...) while((s32[]{:T(128)}, f32[32,128,128]{2,1,0:T(8,128)}, ...), condition=%wide.region_6.7_spmd.clone, body=%wide.region_4.6_spmd.clone.sunk | while | flops 270534272 | bytes 33626048 | solution.py:74
  30.4 1.0 gather_fusion.1
  31.3 4.4 %fusion.25 = f32[64,128,128]{2,1,0:T(8,128)} fusion(bf16[64,128,128]{2,1,0:T(8,128)(2,1)S(1)} %gather_fusion.1, bf16[320,128,128]{1,2,0:T(8,128)(2,1)} %get-tuple-element.508, s32[]{:T(128)S(6)} %select_n.64), kind=kOutput, calls=%fused_computation.12.clone.1 | convolution fusion | flops 268435456 | bytes 8388612 | tf_op jit(solution)/shard_map/while/body/eval_jaxpr/tab,taf->tbf/dot_general | solution.py:65
  36.0 8.8 %scatter_fusion.1 = f32[33,128,128]{2,1,0:T(8,128)S(1)} fusion(f32[33,128,128]{2,1,0:T(8,128)S(1)} %broadcast.112, s32[64]{0:T(128)S(1)} %get-tuple-element.442, f32[64,128,128]{2,1,0:T(8,128)} %fusion.25), kind=kCustom, calls=%fused_computation.3.clone.clone.1 | custom fusion | flops 1048576 | bytes 12583168 | tf_op jit(solution)/shard_map/while/body/eval_jaxpr/scatter-add | solution.py:70
  44.8 1.7 slice_add_fusion.5
  47.2 1.0 gather_fusion.1
  48.1 4.4 %fusion.25 = f32[64,128,128]{2,1,0:T(8,128)} fusion(bf16[64,128,128]{2,1,0:T(8,128)(2,1)S(1)} %gather_fusion.1, bf16[320,128,128]{1,2,0:T(8,128)(2,1)} %get-tuple-element.508, s32[]{:T(128)S(6)} %select_n.64), kind=kOutput, calls=%fused_computation.12.clone.1 | convolution fusion | flops 268435456 | bytes 8388612 | tf_op jit(solution)/shard_map/while/body/eval_jaxpr/tab,taf->tbf/dot_general | solution.py:65
  52.8 8.8 %scatter_fusion.1 = f32[33,128,128]{2,1,0:T(8,128)S(1)} fusion(f32[33,128,128]{2,1,0:T(8,128)S(1)} %broadcast.112, s32[64]{0:T(128)S(1)} %get-tuple-element.442, f32[64,128,128]{2,1,0:T(8,128)} %fusion.25), kind=kCustom, calls=%fused_computation.3.clone.clone.1 | custom fusion | flops 1048576 | bytes 12583168 | tf_op jit(solution)/shard_map/while/body/eval_jaxpr/scatter-add | solution.py:70
  61.6 3.2 %slice_add_fusion.5 = f32[32,128,128]{2,1,0:T(8,128)} fusion(f32[33,128,128]{2,1,0:T(8,128)S(1)} %scatter_fusion.1, f32[32,128,128]{2,1,0:T(8,128)} %get-tuple-element.493, pred[]{:T(512)S(6)} %compare.7), kind=kLoop, calls=%fused_computation.11.clone.1 | loop fusion | flops 1048576 | bytes 6291457 | tf_op jit(solution)/shard_map/while/body/eval_jaxpr/add | solution.py:71
  65.6 1.0 gather_fusion.1
  66.5 4.4 %fusion.25 = f32[64,128,128]{2,1,0:T(8,128)} fusion(bf16[64,128,128]{2,1,0:T(8,128)(2,1)S(1)} %gather_fusion.1, bf16[320,128,128]{1,2,0:T(8,128)(2,1)} %get-tuple-element.508, s32[]{:T(128)S(6)} %select_n.64), kind=kOutput, calls=%fused_computation.12.clone.1 | convolution fusion | flops 268435456 | bytes 8388612 | tf_op jit(solution)/shard_map/while/body/eval_jaxpr/tab,taf->tbf/dot_general | solution.py:65
  71.2 8.8 %scatter_fusion.1 = f32[33,128,128]{2,1,0:T(8,128)S(1)} fusion(f32[33,128,128]{2,1,0:T(8,128)S(1)} %broadcast.112, s32[64]{0:T(128)S(1)} %get-tuple-element.442, f32[64,128,128]{2,1,0:T(8,128)} %fusion.25), kind=kCustom, calls=%fused_computation.3.clone.clone.1 | custom fusion | flops 1048576 | bytes 12583168 | tf_op jit(solution)/shard_map/while/body/eval_jaxpr/scatter-add | solution.py:70
  80.0 3.2 %slice_add_fusion.5 = f32[32,128,128]{2,1,0:T(8,128)} fusion(f32[33,128,128]{2,1,0:T(8,128)S(1)} %scatter_fusion.1, f32[32,128,128]{2,1,0:T(8,128)} %get-tuple-element.493, pred[]{:T(512)S(6)} %compare.7), kind=kLoop, calls=%fused_computation.11.clone.1 | loop fusion | flops 1048576 | bytes 6291457 | tf_op jit(solution)/shard_map/while/body/eval_jaxpr/add | solution.py:71
  83.9 1.0 gather_fusion.1
  84.9 4.4 %fusion.25 = f32[64,128,128]{2,1,0:T(8,128)} fusion(bf16[64,128,128]{2,1,0:T(8,128)(2,1)S(1)} %gather_fusion.1, bf16[320,128,128]{1,2,0:T(8,128)(2,1)} %get-tuple-element.508, s32[]{:T(128)S(6)} %select_n.64), kind=kOutput, calls=%fused_computation.12.clone.1 | convolution fusion | flops 268435456 | bytes 8388612 | tf_op jit(solution)/shard_map/while/body/eval_jaxpr/tab,taf->tbf/dot_general | solution.py:65
  89.5 8.8 %scatter_fusion.1 = f32[33,128,128]{2,1,0:T(8,128)S(1)} fusion(f32[33,128,128]{2,1,0:T(8,128)S(1)} %broadcast.112, s32[64]{0:T(128)S(1)} %get-tuple-element.442, f32[64,128,128]{2,1,0:T(8,128)} %fusion.25), kind=kCustom, calls=%fused_computation.3.clone.clone.1 | custom fusion | flops 1048576 | bytes 12583168 | tf_op jit(solution)/shard_map/while/body/eval_jaxpr/scatter-add | solution.py:70
  98.3 3.2 %slice_add_fusion.5 = f32[32,128,128]{2,1,0:T(8,128)} fusion(f32[33,128,128]{2,1,0:T(8,128)S(1)} %scatter_fusion.1, f32[32,128,128]{2,1,0:T(8,128)} %get-tuple-element.493, pred[]{:T(512)S(6)} %compare.7), kind=kLoop, calls=%fused_computation.11.clone.1 | loop fusion | flops 1048576 | bytes 6291457 | tf_op jit(solution)/shard_map/while/body/eval_jaxpr/add | solution.py:71
  102.3 1.0 gather_fusion.1
  103.3 4.4 %fusion.25 = f32[64,128,128]{2,1,0:T(8,128)} fusion(bf16[64,128,128]{2,1,0:T(8,128)(2,1)S(1)} %gather_fusion.1, bf16[320,128,128]{1,2,0:T(8,128)(2,1)} %get-tuple-element.508, s32[]{:T(128)S(6)} %select_n.64), kind=kOutput, calls=%fused_computation.12.clone.1 | convolution fusion | flops 268435456 | bytes 8388612 | tf_op jit(solution)/shard_map/while/body/eval_jaxpr/tab,taf->tbf/dot_general | solution.py:65
  107.9 8.8 %scatter_fusion.1 = f32[33,128,128]{2,1,0:T(8,128)S(1)} fusion(f32[33,128,128]{2,1,0:T(8,128)S(1)} %broadcast.112, s32[64]{0:T(128)S(1)} %get-tuple-element.442, f32[64,128,128]{2,1,0:T(8,128)} %fusion.25), kind=kCustom, calls=%fused_computation.3.clone.clone.1 | custom fusion | flops 1048576 | bytes 12583168 | tf_op jit(solution)/shard_map/while/body/eval_jaxpr/scatter-add | solution.py:70
  116.7 3.2 %slice_add_fusion.5 = f32[32,128,128]{2,1,0:T(8,128)} fusion(f32[33,128,128]{2,1,0:T(8,128)S(1)} %scatter_fusion.1, f32[32,128,128]{2,1,0:T(8,128)} %get-tuple-element.493, pred[]{:T(512)S(6)} %compare.7), kind=kLoop, calls=%fused_computation.11.clone.1 | loop fusion | flops 1048576 | bytes 6291457 | tf_op jit(solution)/shard_map/while/body/eval_jaxpr/add | solution.py:71
  120.1 2.3 convolution_convert_fusion
  122.4 74.4 %while.28 = (s32[]{:T(128)}, f32[4,128,128]{2,1,0:T(8,128)S(1)}, s32[]{:T(128)}, s32[320]{0:T(512)S(1)}, bf16[320,128,128]{2,1,0:T(8,128)(2,1)}, /*index=5*/s32[...) while((s32[]{:T(128)}, f32[4,128,128]{2,1,0:T(8,128)S(1)}, ...), condition=%wide.region_2.3_spmd.clone, body=%wide.region_0.2_spmd.clone.sunk | while | flops 269616512 | bytes 26286016 | solution.py:47
  123.1 1.0 gather_fusion
  124.1 4.2 %fusion.22 = f32[64,128,128]{2,1,0:T(8,128)} fusion(bf16[64,128,128]{2,1,0:T(8,128)(2,1)S(1)} %gather_fusion, bf16[320,128,128]{2,1,0:T(8,128)(2,1)} %get-tuple-element.472, s32[]{:T(128)S(6)} %select_n.62), kind=kOutput, calls=%fused_computation.4.clone.1 | convolution fusion | flops 268435456 | bytes 8388612 | tf_op jit(solution)/shard_map/while/body/eval_jaxpr/tab,tbf->taf/dot_general | solution.py:40
  128.3 8.9 %scatter_fusion = f32[5,128,128]{2,1,0:T(8,128)S(1)} fusion(f32[5,128,128]{2,1,0:T(8,128)S(1)} %broadcast.105, s32[64]{0:T(128)S(1)} %get-tuple-element.433, f32[64,128,128]{2,1,0:T(8,128)} %fusion.22), kind=kCustom, calls=%fused_computation.2.clone.clone.1 | custom fusion | flops 1048576 | bytes 12583168 | tf_op jit(solution)/shard_map/while/body/eval_jaxpr/scatter-add | solution.py:44
  138.1 1.0 gather_fusion
  139.1 4.3 %fusion.22 = f32[64,128,128]{2,1,0:T(8,128)} fusion(bf16[64,128,128]{2,1,0:T(8,128)(2,1)S(1)} %gather_fusion, bf16[320,128,128]{2,1,0:T(8,128)(2,1)} %get-tuple-element.472, s32[]{:T(128)S(6)} %select_n.62), kind=kOutput, calls=%fused_computation.4.clone.1 | convolution fusion | flops 268435456 | bytes 8388612 | tf_op jit(solution)/shard_map/while/body/eval_jaxpr/tab,tbf->taf/dot_general | solution.py:40
  143.4 8.8 %scatter_fusion = f32[5,128,128]{2,1,0:T(8,128)S(1)} fusion(f32[5,128,128]{2,1,0:T(8,128)S(1)} %broadcast.105, s32[64]{0:T(128)S(1)} %get-tuple-element.433, f32[64,128,128]{2,1,0:T(8,128)} %fusion.22), kind=kCustom, calls=%fused_computation.2.clone.clone.1 | custom fusion | flops 1048576 | bytes 12583168 | tf_op jit(solution)/shard_map/while/body/eval_jaxpr/scatter-add | solution.py:44
  153.0 1.0 gather_fusion
  154.0 4.2 %fusion.22 = f32[64,128,128]{2,1,0:T(8,128)} fusion(bf16[64,128,128]{2,1,0:T(8,128)(2,1)S(1)} %gather_fusion, bf16[320,128,128]{2,1,0:T(8,128)(2,1)} %get-tuple-element.472, s32[]{:T(128)S(6)} %select_n.62), kind=kOutput, calls=%fused_computation.4.clone.1 | convolution fusion | flops 268435456 | bytes 8388612 | tf_op jit(solution)/shard_map/while/body/eval_jaxpr/tab,tbf->taf/dot_general | solution.py:40
  158.2 8.8 %scatter_fusion = f32[5,128,128]{2,1,0:T(8,128)S(1)} fusion(f32[5,128,128]{2,1,0:T(8,128)S(1)} %broadcast.105, s32[64]{0:T(128)S(1)} %get-tuple-element.433, f32[64,128,128]{2,1,0:T(8,128)} %fusion.22), kind=kCustom, calls=%fused_computation.2.clone.clone.1 | custom fusion | flops 1048576 | bytes 12583168 | tf_op jit(solution)/shard_map/while/body/eval_jaxpr/scatter-add | solution.py:44
  167.9 1.0 gather_fusion
  168.8 4.2 %fusion.22 = f32[64,128,128]{2,1,0:T(8,128)} fusion(bf16[64,128,128]{2,1,0:T(8,128)(2,1)S(1)} %gather_fusion, bf16[320,128,128]{2,1,0:T(8,128)(2,1)} %get-tuple-element.472, s32[]{:T(128)S(6)} %select_n.62), kind=kOutput, calls=%fused_computation.4.clone.1 | convolution fusion | flops 268435456 | bytes 8388612 | tf_op jit(solution)/shard_map/while/body/eval_jaxpr/tab,tbf->taf/dot_general | solution.py:40
  173.1 8.8 %scatter_fusion = f32[5,128,128]{2,1,0:T(8,128)S(1)} fusion(f32[5,128,128]{2,1,0:T(8,128)S(1)} %broadcast.105, s32[64]{0:T(128)S(1)} %get-tuple-element.433, f32[64,128,128]{2,1,0:T(8,128)} %fusion.22), kind=kCustom, calls=%fused_computation.2.clone.clone.1 | custom fusion | flops 1048576 | bytes 12583168 | tf_op jit(solution)/shard_map/while/body/eval_jaxpr/scatter-add | solution.py:44
  182.7 1.0 gather_fusion
  183.7 4.2 %fusion.22 = f32[64,128,128]{2,1,0:T(8,128)} fusion(bf16[64,128,128]{2,1,0:T(8,128)(2,1)S(1)} %gather_fusion, bf16[320,128,128]{2,1,0:T(8,128)(2,1)} %get-tuple-element.472, s32[]{:T(128)S(6)} %select_n.62), kind=kOutput, calls=%fused_computation.4.clone.1 | convolution fusion | flops 268435456 | bytes 8388612 | tf_op jit(solution)/shard_map/while/body/eval_jaxpr/tab,tbf->taf/dot_general | solution.py:40
  187.9 8.8 %scatter_fusion = f32[5,128,128]{2,1,0:T(8,128)S(1)} fusion(f32[5,128,128]{2,1,0:T(8,128)S(1)} %broadcast.105, s32[64]{0:T(128)S(1)} %get-tuple-element.433, f32[64,128,128]{2,1,0:T(8,128)} %fusion.22), kind=kCustom, calls=%fused_computation.2.clone.clone.1 | custom fusion | flops 1048576 | bytes 12583168 | tf_op jit(solution)/shard_map/while/body/eval_jaxpr/scatter-add | solution.py:44
  197.6 1.8 convolution_bitcast_fusion
  199.4 1.7 convolution_convert_fusion.1
  201.2 10.3 %reduce-scatter.3.cloned.1.call-done = f32[256,128]{1,0:T(8,128)} async-done(((f32[512,128]{1,0:T(8,128)}), f32[256,128]{1,0:T(8,128)}) %reduce-scatter.3.cloned.1.call-update) | async-done | bytes 131088 | tf_op jit(solution)/shard_map/reduce_scatter | solution.py:53
  211.5 1.5 convert_element_type.13
  213.1 64.9 %all-gather.6.cloned.1.call-done = f32[8192,128]{0,1:T(8,128)} async-done(((f32[256,128]{0,1:T(8,128)}), f32[8192,128]{0,1:T(8,128)}) %all-gather.6.cloned.1.call-update) | async-done | bytes 4194320 | tf_op jit(solution)/shard_map/all_gather | solution.py:88
  278.0 3.5 %copy.16 = f32[16,8,32,256]{3,2,1,0:T(8,128)S(1)} copy(f32[16,8,32,256]{3,1,2,0:T(8,128)} %bitcast.30) | data formatting | bytes 8388608
  281.5 1.0 bitcast_reduce_fusion
  282.5 0.8 copy.14
  (56 shorter events, 12.0 us)
Async XLA Ops:
  7.2 112.9 %copy-start = (bf16[256,128]{1,0:T(8,128)(2,1)S(1)}, bf16[256,128]{1,0:T(8,128)(2,1)}, u32[]{:S(2)}) copy-start(bf16[256,128]{1,0:T(8,128)(2,1)} %param.12) | copy-start | bytes 196612
  7.2 112.9 %all-gather.4.cloned.1.call-start = ((), (), s32[]{:S(2)}) async-start(), calls=%async_computation.2 | async-start | bytes 2228224 | tf_op jit(solution)/shard_map/all_gather | solution.py:24
  7.9 189.7 %reduce-scatter.5.cloned.1.call-start = ((), (), s32[]{:S(2)}) async-start(), calls=%async_computation.4 | async-start | bytes 2228224 | tf_op jit(solution)/shard_map/reduce_scatter | solution.py:77
  9.4 14.4 %copy-start.2 = (bf16[256,128]{1,0:T(8,128)(2,1)S(1)}, bf16[256,128]{1,0:T(8,128)(2,1)}, u32[]{:S(2)}) copy-start(bf16[256,128]{1,0:T(8,128)(2,1)} %param.17) | copy-start | bytes 196612
  120.0 91.5 %reduce-scatter.3.cloned.1.call-start = ((), (), s32[]{:S(2)}) async-start(), calls=%async_computation.3 | async-start | bytes 393216 | tf_op jit(solution)/shard_map/reduce_scatter | solution.py:53
  196.8 0.7 copy-start.1
  197.5 80.5 %all-gather.6.cloned.1.call-start = ((), (), s32[]{:S(2)}) async-start(), calls=%async_computation.5 | async-start | bytes 4325376 | tf_op jit(solution)/shard_map/all_gather | solution.py:88
Sparse Core Ops, SparseCore 0:
  10.1 44.1 all-gather.3
  120.1 63.6 reduce-scatter.4
  197.6 13.8 reduce-scatter.2
  214.8 63.1 all-gather.5
